TPU v7x, 128 devices: a whole 4x4x4 slice. The times are simulated.
128 devices in a mesh: row: 8 (over x, core), col: 16 (over z, y).
Axes of the slice: x: 4, y: 4, z: 4, core: 2. Of those that a mesh axis runs over, the one named last changes fastest.
Arguments:
- features: float32 [32768, 128], P('col', 'row'), may hold values from -6 to 6
- tile_rows: int32 [8, 16, 80], P('row', 'col'), may hold values from 0 to 32, as said below
- tile_cols: int32 [8, 16, 80], P('row', 'col'), may hold values from 0 to 15
- tile_values: float32 [8, 16, 80, 128, 128], P('row', 'col'), may hold values from -0.51881118 to 0.51881118, as said below
- weight_in: float32 [128, 256], replicated, may hold values from -0.5 to 0.5
- weight_out: float32 [256, 256], replicated, may hold values from -0.375 to 0.375
- cotangent: float32 [32768, 256], P(('col', 'row')), may hold values from -0.03125 to 0.03125
Outputs:
- output: float32 [32768, 256], P(('col', 'row'))
- grad_in: float32 [128, 256], replicated
- grad_out: float32 [256, 256], replicated
Inputs may be any that keep to these rules, and one draw needn't show every extreme that they name: `tile_rows`: slot s of device (i, j) is used for s below that device's tile count and holds a tile row 0 to 31; unused slots hold 32. Used slots come first, no (row, column) pair repeats within a device, and in every draw some device uses all 80 slots. `tile_values`: A tile is sparse: each entry is nonzero with probability 2.56 / 128, at random positions.
All inputs are finite; a program needn't handle non-finite values.
Results may differ from a plain program's by a relative error of at most 0.0003.
Values sent between devices are 32-bit elements; how exact they have to be, the bound alone decides.
A program may use at most 128 MiB of HBM per device.

v0:
```python
import jax
import jax.numpy as jnp
from jax import lax
from jax.sharding import PartitionSpec as P

TILE = 128


def forward_tiles(gathered, tile_row, tile_col, tile_block, out_tiles):
    width = gathered.shape[1]
    blocks = gathered.reshape(-1, TILE, width)
    picked = jnp.take(blocks, tile_col, axis=0)
    products = jnp.einsum("tab,tbf->taf", tile_block, picked, precision=lax.Precision.HIGHEST)
    onehot = (tile_row[None, :] == jnp.arange(out_tiles, dtype=jnp.int32)[:, None]).astype(
        jnp.float32
    )
    summed = jnp.einsum("rt,taf->raf", onehot, products, precision=lax.Precision.HIGHEST)
    return summed.reshape(out_tiles * TILE, width)


def adjoint_tiles(row_grads, tile_row, tile_col, tile_block, out_tiles):
    width = row_grads.shape[1]
    in_tiles = row_grads.shape[0] // TILE
    blocks = row_grads.reshape(in_tiles, TILE, width)
    picked = jnp.take(blocks, jnp.minimum(tile_row, in_tiles - 1), axis=0)
    products = jnp.einsum("tba,tbf->taf", tile_block, picked, precision=lax.Precision.HIGHEST)
    matches = tile_col[None, :] == jnp.arange(out_tiles, dtype=jnp.int32)[:, None]
    onehot = (matches & (tile_row < in_tiles)[None, :]).astype(jnp.float32)
    summed = jnp.einsum("rt,taf->raf", onehot, products, precision=lax.Precision.HIGHEST)
    return summed.reshape(out_tiles * TILE, width)


def dense_product(left, right):
    return jnp.dot(left, right, precision=lax.Precision.HIGHEST, preferred_element_type=jnp.float32)


def inner_rows(left, right):
    return lax.dot_general(
        left,
        right,
        (((0,), (0,)), ((), ())),
        precision=lax.Precision.HIGHEST,
        preferred_element_type=jnp.float32,
    )


def per_device(features, tile_rows, tile_cols, tile_values, weight_in, weight_out, cotangent):
    tile_row = tile_rows.reshape(-1)
    tile_col = tile_cols.reshape(-1)
    tile_block = tile_values.reshape(-1, TILE, TILE)
    local_rows = cotangent.shape[0]
    row_tiles = lax.axis_size("col") * local_rows // TILE
    col_tiles = lax.axis_size("row") * local_rows // TILE
    x_local = lax.all_to_all(features, "row", split_axis=0, concat_axis=1, tiled=True)
    support = dense_product(x_local, weight_in)
    gathered = lax.all_gather(support, "row", axis=0, tiled=True)
    partial_one = forward_tiles(gathered, tile_row, tile_col, tile_block, row_tiles)
    pre_act = lax.psum_scatter(partial_one, "col", scatter_dimension=0, tiled=True)
    hidden = jax.nn.silu(pre_act)
    support_two = dense_product(hidden, weight_out)
    gathered_two = lax.all_gather(support_two, "row", axis=0, tiled=True)
    partial_two = forward_tiles(gathered_two, tile_row, tile_col, tile_block, row_tiles)
    output = lax.psum_scatter(partial_two, "col", scatter_dimension=0, tiled=True)
    rows_out = lax.all_gather(cotangent, "col", axis=0, tiled=True)
    adjoint_two = adjoint_tiles(rows_out, tile_row, tile_col, tile_block, col_tiles)
    d_support_two = lax.psum_scatter(adjoint_two, "row", scatter_dimension=0, tiled=True)
    grad_out_local = inner_rows(hidden, d_support_two)
    d_hidden = dense_product(d_support_two, weight_out.T)
    sigmoid_pre = jax.nn.sigmoid(pre_act)
    d_pre = d_hidden * sigmoid_pre * (1.0 + pre_act * (1.0 - sigmoid_pre))
    rows_in = lax.all_gather(d_pre, "col", axis=0, tiled=True)
    adjoint_one = adjoint_tiles(rows_in, tile_row, tile_col, tile_block, col_tiles)
    d_support = lax.psum_scatter(adjoint_one, "row", scatter_dimension=0, tiled=True)
    grad_in_local = inner_rows(x_local, d_support)
    grad_in, grad_out = lax.psum((grad_in_local, grad_out_local), ("row", "col"))
    return (output, grad_in, grad_out)


def solution(mesh):
    return jax.shard_map(
        per_device,
        mesh=mesh,
        in_specs=(
            P("col", "row"),
            P("row", "col", None),
            P("row", "col", None),
            P("row", "col", None, None, None),
            P(),
            P(),
            P(("col", "row"), None),
        ),
        out_specs=(P(("col", "row"), None), P(), P()),
        check_vma=False,
    )
```

profile of v0, /device:TPU:0, one launch (start us, length us, event | category | flops | bytes accessed | tf_op | source)
XLA Modules:
  0.0 643.5 jit_solution(13298213714380566996)
XLA Ops:
  7.2 0.0 all-gather.9.cloned.1.call-start
  7.2 0.7 all-gather.9.cloned.1.call-update
  7.9 0.0 all-gather.5.cloned.1.call-start
  8.0 0.9 copy.60
  8.9 10.3 %all_to_all.19 = f32[8,256,16]{1,2,0:T(8,128)S(1)} all-to-all(f32[8,256,16]{1,2,0:T(8,128)S(1)} %bitcast.80), channel_id=1, replica_groups=mesh['row'=8,'col'=16] {'row'}, dimensions={0} | all-to-all | bytes 262144 | tf_op jit(solution)/shard_map/all_to_all | solution.py:54
  19.2 2.0 fusion.69
  21.2 0.0 all-gather.5.cloned.1.call-update
  21.2 0.0 reduce-scatter.9.cloned.1.call-start
  21.3 0.7 compare_and_fusion
  22.0 42.2 %all-gather.9.cloned.1.call-done = f32[4096,256]{1,0:T(8,128)} async-done(((f32[256,256]{1,0:T(8,128)}), f32[4096,256]{1,0:T(8,128)}) %all-gather.9.cloned.1.call-update) | async-done | bytes 4194320 | tf_op jit(solution)/shard_map/all_gather | solution.py:64
  64.2 9.9 %gather_fusion.2 = f32[80,128,256]{2,1,0:T(8,128)} fusion(f32[32,128,256]{2,1,0:T(8,128)} %bitcast.72, s32[1024]{0:T(1024)S(1)} %pad_clamp_fusion), kind=kCustom, calls=%fused_computation.1.clone | custom fusion | bytes 20971840 | tf_op jit(solution)/shard_map/jit(_take)/gather | solution.py:25
  74.0 23.1 %fusion.30 = f32[80,128,256]{1,2,0:T(8,128)} fusion(f32[1,1,80,128,128]{4,3,2,1,0:T(8,128)} %param.14, f32[80,128,256]{2,1,0:T(8,128)} %gather_fusion.2, pred[80]{0:T(512)(128)(4,1)S(1)} %get-tuple-element.22), kind=kOutput, calls=%fused_computation.26 | convolution fusion | flops 4029153280 | bytes 26214480 | tf_op jit(solution)/shard_map/tba,tbf->taf/dot_general | solution.py:26
  97.2 11.6 %copy.48 = f32[80,128,256]{2,0,1:T(8,128)} copy(f32[80,128,256]{1,2,0:T(8,128)} %fusion.30) | data formatting | bytes 20971520 | tf_op jit(solution)/shard_map/tba,tbf->taf/dot_general | solution.py:26
  108.8 6.2 fusion.57
  115.1 2.6 copy.49
  117.7 0.4 reduce-scatter.5.cloned.1.call-start
  118.1 0.0 all-gather.5.cloned.1.call-done
  118.1 9.9 %gather_fusion = f32[80,128,256]{2,1,0:T(8,128)} fusion(f32[16,128,256]{2,1,0:T(8,128)} %bitcast.70, s32[1024]{0:T(1024)S(1)} %pad_clamp_fusion.1), kind=kCustom, calls=%fused_computation.clone | custom fusion | bytes 20971840 | tf_op jit(solution)/shard_map/jit(_take)/gather | solution.py:12
  128.0 23.0 %fusion.20 = f32[80,128,256]{1,2,0:T(8,128)} fusion(f32[1,1,80,128,128]{4,3,2,1,0:T(8,128)} %param.14, f32[80,128,256]{2,1,0:T(8,128)} %gather_fusion, pred[80]{0:T(512)(128)(4,1)S(1)} %compare_and_fusion.1), kind=kOutput, calls=%fused_computation.24 | convolution fusion | flops 4029153280 | bytes 26214480 | tf_op jit(solution)/shard_map/tab,tbf->taf/dot_general | solution.py:13
  151.0 11.7 %copy.42 = f32[80,128,256]{2,0,1:T(8,128)} copy(f32[80,128,256]{1,2,0:T(8,128)} %fusion.20) | data formatting | bytes 20971520 | tf_op jit(solution)/shard_map/tab,tbf->taf/dot_general | solution.py:13
  162.7 6.9 %fusion.49 = f32[32,128,256]{2,0,1:T(8,128)S(1)} fusion(f32[80,128,256]{2,0,1:T(8,128)} %copy.42, s32[80]{0:T(128)S(1)} %bitcast.82), kind=kOutput, calls=%fused_computation.39 | convolution fusion | flops 1006635520 | bytes 14680384 | tf_op jit(solution)/shard_map/rt,taf->raf/dot_general | solution.py:17
  169.6 4.4 copy.43
  174.0 0.0 all-gather.11.cloned.1.call-start
  174.0 0.0 reduce-scatter.9.cloned.1.call-done
  174.0 78.6 %reduce-scatter.5.cloned.1.call-done = f32[256,256]{1,0:T(8,128)} async-done(((f32[4096,256]{1,0:T(8,128)}), f32[256,256]{1,0:T(8,128)}) %reduce-scatter.5.cloned.1.call-update) | async-done | bytes 262160 | tf_op jit(solution)/shard_map/reduce_scatter | solution.py:58
  252.6 2.1 fusion.40
  254.8 0.0 all-gather.7.cloned.1.call-start
  254.8 2.1 fusion.44
  256.9 0.0 reduce-scatter.11.cloned.1.call-start
  257.0 48.8 %all-gather.11.cloned.1.call-done = f32[4096,256]{1,0:T(8,128)} async-done(((f32[256,256]{1,0:T(8,128)}), f32[4096,256]{1,0:T(8,128)}) %all-gather.11.cloned.1.call-update) | async-done | bytes 4194320 | tf_op jit(solution)/shard_map/all_gather | solution.py:71
  305.8 10.1 %gather_fusion.3 = f32[80,128,256]{2,1,0:T(8,128)} fusion(f32[32,128,256]{2,1,0:T(8,128)} %bitcast.73, s32[1024]{0:T(1024)S(1)} %pad_clamp_fusion), kind=kCustom, calls=%fused_computation.3.clone | custom fusion | bytes 20971840 | tf_op jit(solution)/shard_map/jit(_take)/gather | solution.py:25
  315.8 23.2 %fusion.35 = f32[80,128,256]{1,2,0:T(8,128)} fusion(f32[1,1,80,128,128]{4,3,2,1,0:T(8,128)} %param.14, f32[80,128,256]{2,1,0:T(8,128)} %gather_fusion.3, pred[80]{0:T(512)(128)(4,1)S(1)} %get-tuple-element.22), kind=kOutput, calls=%fused_computation.27 | convolution fusion | flops 4029153280 | bytes 26214480 | tf_op jit(solution)/shard_map/tba,tbf->taf/dot_general | solution.py:26
  339.1 11.6 %copy.51 = f32[80,128,256]{2,0,1:T(8,128)} copy(f32[80,128,256]{1,2,0:T(8,128)} %fusion.35) | data formatting | bytes 20971520 | tf_op jit(solution)/shard_map/tba,tbf->taf/dot_general | solution.py:26
  350.7 6.3 fusion.55
  357.0 2.6 copy.52
  359.6 0.3 all-reduce.3.cloned.1.call-start
  359.9 1.3 fusion.42
  361.2 9.8 %gather_fusion.1 = f32[80,128,256]{2,1,0:T(8,128)} fusion(f32[16,128,256]{2,1,0:T(8,128)} %bitcast.71, s32[1024]{0:T(1024)S(1)} %pad_clamp_fusion.1), kind=kCustom, calls=%fused_computation.2.clone | custom fusion | bytes 20971840 | tf_op jit(solution)/shard_map/jit(_take)/gather | solution.py:12
  371.0 23.0 %fusion.25 = f32[80,128,256]{1,2,0:T(8,128)} fusion(f32[1,1,80,128,128]{4,3,2,1,0:T(8,128)} %param.14, f32[80,128,256]{2,1,0:T(8,128)} %gather_fusion.1, pred[80]{0:T(512)(128)(4,1)S(1)} %compare_and_fusion.1), kind=kOutput, calls=%fused_computation.25 | convolution fusion | flops 4029153280 | bytes 26214480 | tf_op jit(solution)/shard_map/tab,tbf->taf/dot_general | solution.py:13
  394.0 11.6 %copy.45 = f32[80,128,256]{2,0,1:T(8,128)} copy(f32[80,128,256]{1,2,0:T(8,128)} %fusion.25) | data formatting | bytes 20971520 | tf_op jit(solution)/shard_map/tab,tbf->taf/dot_general | solution.py:13
  405.6 2.2 convolution_bitcast_fusion
  407.9 0.3 reduce-scatter.7.cloned.1.call-start
  408.2 6.9 %fusion.47 = f32[32,128,256]{2,0,1:T(8,128)S(1)} fusion(f32[80,128,256]{2,0,1:T(8,128)} %copy.45, s32[80]{0:T(128)S(1)} %bitcast.83), kind=kOutput, calls=%fused_computation.38 | convolution fusion | flops 1006635520 | bytes 14680384 | tf_op jit(solution)/shard_map/rt,taf->raf/dot_general | solution.py:17
  415.1 4.4 copy.46
  419.4 134.7 %all-reduce.3.cloned.1.call-done = (f32[128,256]{0,1:T(8,128)}, f32[256,256]{1,0:T(8,128)}) async-done(((f32[128,256]{0,1:T(8,128)}, f32[256,256]{1,0:T(8,128)}), (f32[128,256]{0,1:T(8,128)}, f32[256,256]{1,0:T(8,128)})) %all-reduce.3.cloned.1.call-update) | async-done | bytes 393232 | tf_op jit(solution)/shard_map/psum | solution.py:75
  554.2 1.7 copy.53
  555.8 79.0 %reduce-scatter.7.cloned.1.call-done = f32[256,256]{1,0:T(8,128)} async-done(((f32[4096,256]{1,0:T(8,128)}), f32[256,256]{1,0:T(8,128)}) %reduce-scatter.7.cloned.1.call-update) | async-done | bytes 262160 | tf_op jit(solution)/shard_map/reduce_scatter | solution.py:63
  634.9 1.7 copy.63
  (25 shorter events, 0.2 us)
Async XLA Ops:
  7.2 245.4 %copy-start = (f32[256,256]{1,0:T(8,128)S(1)}, f32[256,256]{1,0:T(8,128)}, u32[]{:S(2)}) copy-start(f32[256,256]{1,0:T(8,128)} %param.16) | copy-start | bytes 786436
  7.2 57.0 %all-gather.9.cloned.1.call-start = ((), (), s32[]{:S(2)}) async-start(), calls=%async_computation.9 | async-start | bytes 4456448 | tf_op jit(solution)/shard_map/all_gather | solution.py:64
  7.9 110.2 %all-gather.5.cloned.1.call-start = ((), (), s32[]{:S(2)}) async-start(), calls=%async_computation.5 | async-start | bytes 2359296 | tf_op jit(solution)/shard_map/all_gather | solution.py:56
  21.2 152.8 %reduce-scatter.9.cloned.1.call-start = ((), (), s32[]{:S(2)}) async-start(), calls=%async_computation.10 | async-start | bytes 2359296 | tf_op jit(solution)/shard_map/reduce_scatter | solution.py:66
  97.2 11.7 %copy-start.3 = (s32[1,1,80]{2,1,0:T(1,128)S(1)}, s32[1,1,80]{2,1,0:T(1,128)}, u32[]{:S(2)}) copy-start(s32[1,1,80]{2,1,0:T(1,128)} %param.13) | copy-start | bytes 964
  117.7 134.9 %reduce-scatter.5.cloned.1.call-start = ((), (), s32[]{:S(2)}) async-start(), calls=%async_computation.6 | async-start | bytes 4456448 | tf_op jit(solution)/shard_map/reduce_scatter | solution.py:58
  151.0 11.7 %copy-start.2 = (s32[1,1,80]{2,1,0:T(1,128)S(1)}, s32[1,1,80]{2,1,0:T(1,128)}, u32[]{:S(2)}) copy-start(s32[1,1,80]{2,1,0:T(1,128)} %param.12) | copy-start | bytes 964
  174.0 131.8 %all-gather.11.cloned.1.call-start = ((), (), s32[]{:S(2)}) async-start(), calls=%async_computation.11 | async-start | bytes 4456448 | tf_op jit(solution)/shard_map/all_gather | solution.py:71
  254.8 106.4 %all-gather.7.cloned.1.call-start = ((), (), s32[]{:S(2)}) async-start(), calls=%async_computation.7 | async-start | bytes 2359296 | tf_op jit(solution)/shard_map/all_gather | solution.py:61
  256.9 148.7 %reduce-scatter.11.cloned.1.call-start = ((), (), s32[]{:S(2)}) async-start(), calls=%async_computation.12 | async-start | bytes 2359296 | tf_op jit(solution)/shard_map/reduce_scatter | solution.py:73
  350.7 9.2 %copy-start.4 = (f32[256,256]{1,0:T(8,128)S(1)}, f32[256,256]{1,0:T(8,128)}, u32[]{:S(2)}) copy-start(f32[256,256]{1,0:T(8,128)} %reduce-scatter.9.cloned.1.call-done) | copy-start | bytes 786436
  350.7 9.2 %copy-start.5 = (f32[256,256]{1,0:T(8,128)S(1)}, f32[256,256]{1,0:T(8,128)}, u32[]{:S(2)}) copy-start(f32[256,256]{1,0:T(8,128)} %reduce-scatter.5.cloned.1.call-done) | copy-start | bytes 786436
  359.6 194.6 %all-reduce.3.cloned.1.call-start = ((), (), s32[]{:S(2)}) async-start(), calls=%async_computation.13 | async-start | bytes 786432 | tf_op jit(solution)/shard_map/psum | solution.py:75
  407.9 228.7 %copy-start.1 = (f32[256,256]{1,0:T(8,128)S(1)}, f32[256,256]{1,0:T(8,128)}, u32[]{:S(2)}) copy-start(f32[256,256]{1,0:T(8,128)} %param.16) | copy-start | bytes 786436
  407.9 227.0 %reduce-scatter.7.cloned.1.call-start = ((), (), s32[]{:S(2)}) async-start(), calls=%async_computation.8 | async-start | bytes 4456448 | tf_op jit(solution)/shard_map/reduce_scatter | solution.py:63
Sparse Core Ops, SparseCore 0:
  10.1 53.9 all-gather.8
  66.5 24.8 all-gather.4
  117.8 33.6 reduce-scatter.8
  174.1 78.4 reduce-scatter.4
  255.1 50.5 all-gather.10
  307.9 24.8 all-gather.6
  359.7 33.6 reduce-scatter.10
  408.0 146.1 all-reduce.2
  558.1 76.7 reduce-scatter.6
where the time goes:
time: 653 us; the launch traced here: 644 us
  waiting for transfers between devices  384 us (59%)
  matrix products  128 us (20%)
  local copies, waits for them, and re-layouts  104 us (16%)
  between operations  14.4 us (2%)
  blocking collectives  10.3 us (2%)
    psum x1, waiting for transfers between devices, per_device(): lax.psum((grad_in_local, grad_out_local), ('row', 'col'))  135 us
    reduce_scatter x1, waiting for transfers between devices, per_device(): lax.psum_scatter(partial_two, 'col', scatter_dimension=0, tiled=True)  79 us
    reduce_scatter x1, waiting for transfers between devices, per_device(): lax.psum_scatter(partial_one, 'col', scatter_dimension=0, tiled=True)  78.6 us
    all_gather x1, waiting for transfers between devices, per_device(): rows_in = lax.all_gather(d_pre, 'col', axis=0, tiled=True)  48.8 us
    dot_general x2, matrix products, adjoint_tiles(): jnp.einsum('tba,tbf->taf', tile_block, picked, precision=lax.Precision.HI...  46.4 us
    dot_general x2, matrix products, forward_tiles(): jnp.einsum('tab,tbf->taf', tile_block, picked, precision=lax.Precision.HI...  46 us
    all_gather x1, waiting for transfers between devices, per_device(): rows_out = lax.all_gather(cotangent, 'col', axis=0, tiled=True)  42.2 us
    dot_general x2, local copies, waits for them, and re-layouts, forward_tiles(): jnp.einsum('tab,tbf->taf', tile_block, picked, precision=lax.Precision.HI...  23.3 us
  transfers between devices with their start and end apart: 9, of which 5 were waited for; matrix products, arithmetic and copies ran while one was open for 35% of the time, Pallas kernels for 0%

commit v1 on v0

--- a/solution.py
+++ b/solution.py
@@ -61,7 +61,9 @@
     gathered_two = lax.all_gather(support_two, "row", axis=0, tiled=True)
     partial_two = forward_tiles(gathered_two, tile_row, tile_col, tile_block, row_tiles)
     output = lax.psum_scatter(partial_two, "col", scatter_dimension=0, tiled=True)
-    rows_out = lax.all_gather(cotangent, "col", axis=0, tiled=True)
+    rows_out = jnp.concatenate(
+        lax.all_to_all(jnp.stack([cotangent] * lax.axis_size("col")), "col", 0, 0), axis=0
+    )
     adjoint_two = adjoint_tiles(rows_out, tile_row, tile_col, tile_block, col_tiles)
     d_support_two = lax.psum_scatter(adjoint_two, "row", scatter_dimension=0, tiled=True)
     grad_out_local = inner_rows(hidden, d_support_two)

time: 653 us -> 680 us (1.041)
  waiting for transfers between devices: 384 us -> 401 us
  starting transfers between devices: 1.18 us -> 9.24 us
    all_to_all x0 -> x1, waiting for transfers between devices: none -> 61.6 us  [per_device(): lax.all_to_all(jnp.stack([cotangent] * lax.axis_size('col')), 'col', 0, 0)]
    all_gather x1 -> x0, waiting for transfers between devices: 42.2 us -> none  [per_device(): rows_out = lax.all_gather(cotangent, 'col', axis=0, tiled=True)]
    all_to_all x0 -> x1, starting transfers between devices: none -> 8.1 us  [per_device(): lax.all_to_all(jnp.stack([cotangent] * lax.axis_size('col')), 'col', 0, 0)]
  transfers between devices with their start and end apart: 9 -> 9, of which waited for: 5 -> 5; matrix products, arithmetic and copies ran while one was open for 35% -> 34% of each run, Pallas kernels for 0% -> 0%
where the time goes in v1:
time: 680 us; the launch traced here: 670 us
  waiting for transfers between devices  401 us (59%)
  matrix products  127 us (19%)
  local copies, waits for them, and re-layouts  108 us (16%)
  between operations  14.7 us (2%)
  blocking collectives  10.3 us (2%)
  starting transfers between devices  9.24 us (1%)
    psum x1, waiting for transfers between devices, per_device(): lax.psum((grad_in_local, grad_out_local), ('row', 'col'))  135 us
    reduce_scatter x1, waiting for transfers between devices, per_device(): lax.psum_scatter(partial_two, 'col', scatter_dimension=0, tiled=True)  79 us
    reduce_scatter x1, waiting for transfers between devices, per_device(): lax.psum_scatter(partial_one, 'col', scatter_dimension=0, tiled=True)  76.5 us
    all_to_all x1, waiting for transfers between devices, per_device(): lax.all_to_all(jnp.stack([cotangent] * lax.axis_size('col')), 'col', 0, 0)  61.6 us
    all_gather x1, waiting for transfers between devices, per_device(): rows_in = lax.all_gather(d_pre, 'col', axis=0, tiled=True)  48.8 us
    dot_general x2, matrix products, adjoint_tiles(): jnp.einsum('tba,tbf->taf', tile_block, picked, precision=lax.Precision.HI...  46.1 us
    dot_general x2, matrix products, forward_tiles(): jnp.einsum('tab,tbf->taf', tile_block, picked, precision=lax.Precision.HI...  46.1 us
    dot_general x2, local copies, waits for them, and re-layouts, adjoint_tiles(): jnp.einsum('tba,tbf->taf', tile_block, picked, precision=lax.Precision.HI...  23.3 us
  transfers between devices with their start and end apart: 9, of which 5 were waited for; matrix products, arithmetic and copies ran while one was open for 34% of the time, Pallas kernels for 0%

profile of v1, /device:TPU:0, one launch (start us, length us, event | category | flops | bytes accessed | tf_op | source)
XLA Modules:
  0.0 670.0 jit_solution(15980502739268783157)
XLA Ops:
  7.2 1.0 copy.60
  8.2 10.3 %all_to_all.24 = f32[8,256,16]{1,2,0:T(8,128)S(1)} all-to-all(f32[8,256,16]{1,2,0:T(8,128)S(1)} %bitcast.79), channel_id=1, replica_groups=mesh['row'=8,'col'=16] {'row'}, dimensions={0} | all-to-all | bytes 262144 | tf_op jit(solution)/shard_map/all_to_all | solution.py:54
  18.5 3.3 stack.2
  21.8 8.1 %all-to-all-start.1 = ((f32[16,256,256]{2,1,0:T(8,128)}), f32[16,256,256]{2,1,0:T(8,128)}, u32[]{:S(2)}, u32[]{:S(2)}) async-start(f32[16,256,256]{2,1,0:T(8,128)} %stack.2), calls=%async_computation.3 | async-start | bytes 8388608 | tf_op jit(solution)/shard_map/all_to_all | solution.py:65
  29.9 0.0 all-gather.4.cloned.1.call-start
  29.9 1.1 fusion.69
  31.1 0.0 all-gather.4.cloned.1.call-update
  31.1 0.0 reduce-scatter.9.cloned.1.call-start
  31.2 61.6 %all-to-all-done.1 = f32[16,256,256]{2,1,0:T(8,128)} async-done(((f32[16,256,256]{2,1,0:T(8,128)}), f32[16,256,256]{2,1,0:T(8,128)}, u32[]{:S(2)}, u32[]{:S(2)}) %all-to-all-start.1) | async-done | bytes 4194336 | tf_op jit(solution)/shard_map/all_to_all | solution.py:65
  92.8 9.9 %gather_fusion.2 = f32[80,128,256]{2,1,0:T(8,128)} fusion(f32[32,128,256]{2,1,0:T(8,128)} %bitcast.13, s32[1024]{0:T(1024)S(1)} %pad_clamp_fusion), kind=kCustom, calls=%fused_computation.1.clone | custom fusion | bytes 20971840 | tf_op jit(solution)/shard_map/jit(_take)/gather | solution.py:25
  102.6 22.9 %fusion.30 = f32[80,128,256]{1,2,0:T(8,128)} fusion(f32[1,1,80,128,128]{4,3,2,1,0:T(8,128)} %param.14, f32[80,128,256]{2,1,0:T(8,128)} %gather_fusion.2, pred[80]{0:T(512)(128)(4,1)S(1)} %get-tuple-element.22), kind=kOutput, calls=%fused_computation.26 | convolution fusion | flops 4029153280 | bytes 26214480 | tf_op jit(solution)/shard_map/tba,tbf->taf/dot_general | solution.py:26
  125.6 11.6 %copy.48 = f32[80,128,256]{2,0,1:T(8,128)} copy(f32[80,128,256]{1,2,0:T(8,128)} %fusion.30) | data formatting | bytes 20971520 | tf_op jit(solution)/shard_map/tba,tbf->taf/dot_general | solution.py:26
  137.2 6.2 fusion.57
  143.4 2.6 copy.49
  146.0 0.0 reduce-scatter.9.cloned.1.call-update
  146.1 0.4 reduce-scatter.5.cloned.1.call-start
  146.5 0.0 all-gather.4.cloned.1.call-done
  146.5 9.7 %gather_fusion = f32[80,128,256]{2,1,0:T(8,128)} fusion(f32[16,128,256]{2,1,0:T(8,128)} %bitcast.70, s32[1024]{0:T(1024)S(1)} %pad_clamp_fusion.1), kind=kCustom, calls=%fused_computation.clone | custom fusion | bytes 20971840 | tf_op jit(solution)/shard_map/jit(_take)/gather | solution.py:12
  156.2 23.1 %fusion.20 = f32[80,128,256]{1,2,0:T(8,128)} fusion(f32[1,1,80,128,128]{4,3,2,1,0:T(8,128)} %param.14, f32[80,128,256]{2,1,0:T(8,128)} %gather_fusion, pred[80]{0:T(512)(128)(4,1)S(1)} %compare_and_fusion.1), kind=kOutput, calls=%fused_computation.24 | convolution fusion | flops 4029153280 | bytes 26214480 | tf_op jit(solution)/shard_map/tab,tbf->taf/dot_general | solution.py:13
  179.3 11.6 %copy.42 = f32[80,128,256]{2,0,1:T(8,128)} copy(f32[80,128,256]{1,2,0:T(8,128)} %fusion.20) | data formatting | bytes 20971520 | tf_op jit(solution)/shard_map/tab,tbf->taf/dot_general | solution.py:13
  191.0 6.9 %fusion.49 = f32[32,128,256]{2,0,1:T(8,128)S(1)} fusion(f32[80,128,256]{2,0,1:T(8,128)} %copy.42, s32[80]{0:T(128)S(1)} %bitcast.81), kind=kOutput, calls=%fused_computation.39 | convolution fusion | flops 1006635520 | bytes 14680384 | tf_op jit(solution)/shard_map/rt,taf->raf/dot_general | solution.py:17
  197.8 4.4 copy.43
  202.2 0.0 all-gather.8.cloned.1.call-start
  202.3 0.0 reduce-scatter.9.cloned.1.call-done
  202.3 76.5 %reduce-scatter.5.cloned.1.call-done = f32[256,256]{1,0:T(8,128)} async-done(((f32[4096,256]{1,0:T(8,128)}), f32[256,256]{1,0:T(8,128)}) %reduce-scatter.5.cloned.1.call-update) | async-done | bytes 262160 | tf_op jit(solution)/shard_map/reduce_scatter | solution.py:58
  278.8 2.1 fusion.40
  280.9 0.0 all-gather.6.cloned.1.call-start
  281.0 2.1 fusion.44
  283.1 0.0 reduce-scatter.11.cloned.1.call-start
  283.1 48.8 %all-gather.8.cloned.1.call-done = f32[4096,256]{1,0:T(8,128)} async-done(((f32[256,256]{1,0:T(8,128)}), f32[4096,256]{1,0:T(8,128)}) %all-gather.8.cloned.1.call-update) | async-done | bytes 4194320 | tf_op jit(solution)/shard_map/all_gather | solution.py:73
  332.0 10.1 %gather_fusion.3 = f32[80,128,256]{2,1,0:T(8,128)} fusion(f32[32,128,256]{2,1,0:T(8,128)} %bitcast.72, s32[1024]{0:T(1024)S(1)} %pad_clamp_fusion), kind=kCustom, calls=%fused_computation.3.clone | custom fusion | bytes 20971840 | tf_op jit(solution)/shard_map/jit(_take)/gather | solution.py:25
  342.0 23.2 %fusion.35 = f32[80,128,256]{1,2,0:T(8,128)} fusion(f32[1,1,80,128,128]{4,3,2,1,0:T(8,128)} %param.14, f32[80,128,256]{2,1,0:T(8,128)} %gather_fusion.3, pred[80]{0:T(512)(128)(4,1)S(1)} %get-tuple-element.22), kind=kOutput, calls=%fused_computation.27 | convolution fusion | flops 4029153280 | bytes 26214480 | tf_op jit(solution)/shard_map/tba,tbf->taf/dot_general | solution.py:26
  365.2 11.6 %copy.51 = f32[80,128,256]{2,0,1:T(8,128)} copy(f32[80,128,256]{1,2,0:T(8,128)} %fusion.35) | data formatting | bytes 20971520 | tf_op jit(solution)/shard_map/tba,tbf->taf/dot_general | solution.py:26
  376.9 6.3 fusion.55
  383.2 2.6 copy.52
  385.8 0.3 all-reduce.3.cloned.1.call-start
  386.1 1.3 fusion.42
  387.4 9.8 %gather_fusion.1 = f32[80,128,256]{2,1,0:T(8,128)} fusion(f32[16,128,256]{2,1,0:T(8,128)} %bitcast.71, s32[1024]{0:T(1024)S(1)} %pad_clamp_fusion.1), kind=kCustom, calls=%fused_computation.2.clone | custom fusion | bytes 20971840 | tf_op jit(solution)/shard_map/jit(_take)/gather | solution.py:12
  397.2 23.0 %fusion.25 = f32[80,128,256]{1,2,0:T(8,128)} fusion(f32[1,1,80,128,128]{4,3,2,1,0:T(8,128)} %param.14, f32[80,128,256]{2,1,0:T(8,128)} %gather_fusion.1, pred[80]{0:T(512)(128)(4,1)S(1)} %compare_and_fusion.1), kind=kOutput, calls=%fused_computation.25 | convolution fusion | flops 4029153280 | bytes 26214480 | tf_op jit(solution)/shard_map/tab,tbf->taf/dot_general | solution.py:13
  420.2 11.6 %copy.45 = f32[80,128,256]{2,0,1:T(8,128)} copy(f32[80,128,256]{1,2,0:T(8,128)} %fusion.25) | data formatting | bytes 20971520 | tf_op jit(solution)/shard_map/tab,tbf->taf/dot_general | solution.py:13
  431.8 2.2 convolution_bitcast_fusion
  434.1 0.3 reduce-scatter.7.cloned.1.call-start
  434.4 6.9 %fusion.47 = f32[32,128,256]{2,0,1:T(8,128)S(1)} fusion(f32[80,128,256]{2,0,1:T(8,128)} %copy.45, s32[80]{0:T(128)S(1)} %bitcast.82), kind=kOutput, calls=%fused_computation.38 | convolution fusion | flops 1006635520 | bytes 14680384 | tf_op jit(solution)/shard_map/rt,taf->raf/dot_general | solution.py:17
  441.2 4.4 copy.46
  445.6 134.7 %all-reduce.3.cloned.1.call-done = (f32[128,256]{0,1:T(8,128)}, f32[256,256]{1,0:T(8,128)}) async-done(((f32[128,256]{0,1:T(8,128)}, f32[256,256]{1,0:T(8,128)}), (f32[128,256]{0,1:T(8,128)}, f32[256,256]{1,0:T(8,128)})) %all-reduce.3.cloned.1.call-update) | async-done | bytes 393232 | tf_op jit(solution)/shard_map/psum | solution.py:77
  580.3 1.7 copy.53
  582.0 79.0 %reduce-scatter.7.cloned.1.call-done = f32[256,256]{1,0:T(8,128)} async-done(((f32[4096,256]{1,0:T(8,128)}), f32[256,256]{1,0:T(8,128)}) %reduce-scatter.7.cloned.1.call-update) | async-done | bytes 262160 | tf_op jit(solution)/shard_map/reduce_scatter | solution.py:63
  661.1 1.7 copy.63
  (27 shorter events, 0.2 us)
Async XLA Ops:
  7.2 271.6 %copy-start = (f32[256,256]{1,0:T(8,128)S(1)}, f32[256,256]{1,0:T(8,128)}, u32[]{:S(2)}) copy-start(f32[256,256]{1,0:T(8,128)} %param.16) | copy-start | bytes 786436
  7.2 22.8 %copy-start.2 = (f32[128,256]{1,0:T(8,128)S(1)}, f32[128,256]{1,0:T(8,128)}, u32[]{:S(2)}) copy-start(f32[128,256]{1,0:T(8,128)} %param.15) | copy-start | bytes 393220
  7.2 23.9 %copy-start.3 = (s32[1,1,80]{2,1,0:T(1,128)S(1)}, s32[1,1,80]{2,1,0:T(1,128)}, u32[]{:S(2)}) copy-start(s32[1,1,80]{2,1,0:T(1,128)} %param.12) | copy-start | bytes 964
  21.8 71.0 %all-to-all-start.1 = ((f32[16,256,256]{2,1,0:T(8,128)}), f32[16,256,256]{2,1,0:T(8,128)}, u32[]{:S(2)}, u32[]{:S(2)}) async-start(f32[16,256,256]{2,1,0:T(8,128)} %stack.2), calls=%async_computation.3 | async-start | bytes 8388608 | tf_op jit(solution)/shard_map/all_to_all | solution.py:65
  29.9 116.6 %all-gather.4.cloned.1.call-start = ((), (), s32[]{:S(2)}) async-start(), calls=%async_computation.6 | async-start | bytes 2359296 | tf_op jit(solution)/shard_map/all_gather | solution.py:56
  31.1 171.2 %reduce-scatter.9.cloned.1.call-start = ((), (), s32[]{:S(2)}) async-start(), calls=%async_computation.10 | async-start | bytes 2359296 | tf_op jit(solution)/shard_map/reduce_scatter | solution.py:68
  125.6 11.7 %copy-start.4 = (s32[1,1,80]{2,1,0:T(1,128)S(1)}, s32[1,1,80]{2,1,0:T(1,128)}, u32[]{:S(2)}) copy-start(s32[1,1,80]{2,1,0:T(1,128)} %param.13) | copy-start | bytes 964
  146.1 132.7 %reduce-scatter.5.cloned.1.call-start = ((), (), s32[]{:S(2)}) async-start(), calls=%async_computation.7 | async-start | bytes 4456448 | tf_op jit(solution)/shard_map/reduce_scatter | solution.py:58
  202.2 129.7 %all-gather.8.cloned.1.call-start = ((), (), s32[]{:S(2)}) async-start(), calls=%async_computation.11 | async-start | bytes 4456448 | tf_op jit(solution)/shard_map/all_gather | solution.py:73
  280.9 106.4 %all-gather.6.cloned.1.call-start = ((), (), s32[]{:S(2)}) async-start(), calls=%async_computation.8 | async-start | bytes 2359296 | tf_op jit(solution)/shard_map/all_gather | solution.py:61
  283.1 148.7 %reduce-scatter.11.cloned.1.call-start = ((), (), s32[]{:S(2)}) async-start(), calls=%async_computation.12 | async-start | bytes 2359296 | tf_op jit(solution)/shard_map/reduce_scatter | solution.py:75
  376.9 9.2 %copy-start.5 = (f32[256,256]{1,0:T(8,128)S(1)}, f32[256,256]{1,0:T(8,128)}, u32[]{:S(2)}) copy-start(f32[256,256]{1,0:T(8,128)} %reduce-scatter.9.cloned.1.call-done) | copy-start | bytes 786436
  376.9 9.2 %copy-start.6 = (f32[256,256]{1,0:T(8,128)S(1)}, f32[256,256]{1,0:T(8,128)}, u32[]{:S(2)}) copy-start(f32[256,256]{1,0:T(8,128)} %reduce-scatter.5.cloned.1.call-done) | copy-start | bytes 786436
  385.8 194.6 %all-reduce.3.cloned.1.call-start = ((), (), s32[]{:S(2)}) async-start(), calls=%async_computation.13 | async-start | bytes 786432 | tf_op jit(solution)/shard_map/psum | solution.py:77
  434.0 228.7 %copy-start.1 = (f32[256,256]{1,0:T(8,128)S(1)}, f32[256,256]{1,0:T(8,128)}, u32[]{:S(2)}) copy-start(f32[256,256]{1,0:T(8,128)} %param.16) | copy-start | bytes 786436
  434.1 227.0 %reduce-scatter.7.cloned.1.call-start = ((), (), s32[]{:S(2)}) async-start(), calls=%async_computation.9 | async-start | bytes 4456448 | tf_op jit(solution)/shard_map/reduce_scatter | solution.py:63
Sparse Core Ops, SparseCore 0:
  33.0 24.8 all-gather.3
  146.2 31.1 reduce-scatter.8
  202.3 76.3 reduce-scatter.4
  281.3 50.5 all-gather.7
  334.1 24.8 all-gather.5
  385.9 33.6 reduce-scatter.10
  434.2 146.1 all-reduce.2
  584.3 76.7 reduce-scatter.6
